TPU v7x, 32 devices: a whole 2x2x4 slice. The times are simulated.
32 devices in a mesh: row: 2 (over y), col: 16 (over z, x, core).
Axes of the slice: x: 2, y: 2, z: 4, core: 2. Of those that a mesh axis runs over, the one named last changes fastest.
Arguments:
- g_greater: bfloat16 [32, 32, 2, 4096], P('row', 'col'), may hold values from -6 to 6
- g_lesser: bfloat16 [32, 32, 2, 4096], P('row', 'col'), may hold values from -6 to 6
- coupling: float32 [64, 64], replicated, may hold values from 0.5 to 1.5
- partner: int32 [64], replicated, may hold values from 0 to 63, each once
- memory_start: int32 [32], P('row'), may hold values from 0 to 31, as said below
Outputs:
- collision: bfloat16 [32, 4, 2, 4096], P(('row', 'col'))
Inputs may be any that keep to these rules, and one draw needn't show every extreme that they name: partner names every orbital once. memory_start[t] lies between 0 and t.
All inputs are finite; a program needn't handle non-finite values.
Results may differ from a plain program's by a relative error of at most 0.0049.
Values may be sent and summed in bfloat16 or wider, within the bound.
A program may use at most 192 MiB of HBM per device.

v0:
```python
import math

import jax
import jax.numpy as jnp
from jax import lax
from jax.sharding import PartitionSpec as P

TW = 4


def complex_product(left_real, left_imag, right_real, right_imag):
    return (
        left_real * right_real - left_imag * right_imag,
        left_real * right_imag + left_imag * right_real,
    )


def per_device(g_greater, g_lesser, coupling, partner, memory_start):
    tile_rows, tile_cols, components, pair_count = g_greater.shape
    row_count = lax.axis_size("row")
    col_count = lax.axis_size("col")
    orbits = coupling.shape[0]
    blocks = tile_rows // col_count
    window = TW
    layout_shape = (blocks, col_count, row_count, blocks, components, pair_count)
    half_greater, half_lesser = (
        lax.all_to_all(
            g_greater.reshape(layout_shape), "col", split_axis=1, concat_axis=1, tiled=True
        ),
        lax.all_to_all(
            g_lesser.reshape(layout_shape), "col", split_axis=1, concat_axis=1, tiled=True
        ),
    )
    got_greater, got_lesser = (
        lax.all_to_all(half_greater, "row", split_axis=2, concat_axis=2, tiled=True),
        lax.all_to_all(half_lesser, "row", split_axis=2, concat_axis=2, tiled=True),
    )
    split_shape = (blocks, col_count, row_count, blocks, components, orbits, orbits)
    flip_greater = (
        got_greater.reshape(split_shape)
        .transpose(3, 1, 2, 0, 4, 6, 5)
        .reshape(tile_rows, tile_cols, components, pair_count)
    )
    flip_lesser = (
        got_lesser.reshape(split_shape)
        .transpose(3, 1, 2, 0, 4, 6, 5)
        .reshape(tile_rows, tile_cols, components, pair_count)
    )
    permuted = (partner[:, None] * orbits + partner[None, :]).reshape(pair_count)
    weight = coupling.reshape(pair_count)
    perm_greater = jnp.take(g_greater, permuted, axis=3)
    perm_lesser = jnp.take(g_lesser, permuted, axis=3)

    def energy(direct, partnered, mirrored):
        first_pair = complex_product(
            direct[:, :, 0].astype(jnp.float32),
            direct[:, :, 1].astype(jnp.float32),
            partnered[:, :, 0].astype(jnp.float32),
            partnered[:, :, 1].astype(jnp.float32),
        )
        triple = complex_product(
            first_pair[0],
            first_pair[1],
            mirrored[:, :, 0].astype(jnp.float32),
            mirrored[:, :, 1].astype(jnp.float32),
        )
        return (weight * triple[0], weight * triple[1])

    greater_sig = energy(g_greater, perm_greater, flip_lesser)
    lesser_sig = energy(g_lesser, perm_lesser, flip_greater)
    first_times = lax.axis_index("row") * tile_rows + jnp.arange(tile_rows, dtype=jnp.int32)
    second_times = jnp.arange(tile_cols, dtype=jnp.int32) * col_count + lax.axis_index("col")
    live_mask = (second_times[None, :] >= memory_start[:, None]) & (
        second_times[None, :] <= first_times[:, None]
    )
    live_mask = live_mask[:, :, None]
    ret_real = jnp.where(live_mask, greater_sig[0] - lesser_sig[0], 0.0).astype(jnp.bfloat16)
    ret_imag = jnp.where(live_mask, greater_sig[1] - lesser_sig[1], 0.0).astype(jnp.bfloat16)
    retarded = jnp.stack([ret_real, ret_imag], axis=2).reshape(
        tile_rows, tile_cols, 2, orbits, orbits
    )
    left_matrix = retarded.transpose(0, 3, 2, 1, 4).reshape(
        tile_rows, orbits, 2 * tile_cols * orbits
    )
    lesser_slab = flip_lesser[:window].reshape(window, tile_cols, 2, orbits, orbits)
    slab_real = (
        lesser_slab[:, :, 0].transpose(1, 3, 0, 2).reshape(tile_cols * orbits, window * orbits)
    )
    slab_imag = (
        lesser_slab[:, :, 1].transpose(1, 3, 0, 2).reshape(tile_cols * orbits, window * orbits)
    )
    upper_half = jnp.concatenate([slab_real, slab_imag], axis=1)
    lower_half = jnp.concatenate([-slab_imag, slab_real], axis=1)
    right_matrix = jnp.concatenate([upper_half, lower_half], axis=0)
    product = jnp.dot(
        left_matrix.reshape(lax.axis_size("col") * blocks * orbits, 2 * tile_cols * orbits),
        right_matrix,
        preferred_element_type=jnp.float32,
    )
    summed = lax.psum_scatter(
        product.reshape(lax.axis_size("col") * blocks, orbits * 2 * window * orbits),
        "col",
        scatter_dimension=0,
        tiled=True,
    )
    scaling = 1.0 / (4.0 * math.sqrt(orbits * tile_rows * row_count))
    summed = summed.reshape(blocks, orbits, 2, window, orbits) * scaling
    return (
        summed.transpose(0, 3, 2, 1, 4).reshape(blocks, window, 2, pair_count).astype(jnp.bfloat16)
    )


def solution(mesh):
    return jax.shard_map(
        per_device,
        mesh=mesh,
        in_specs=(P("row", "col", None, None), P("row", "col", None, None), P(), P(), P("row")),
        out_specs=P(("row", "col"), None, None, None),
        check_vma=False,
    )
```

profile of v0, /device:TPU:30, one launch (start us, length us, event | category | flops | bytes accessed | tf_op | source)
XLA Modules:
  0.0 288.7 jit_solution(657138697506831015)
XLA Ops:
  6.5 6.1 %all-to-all-start = ((bf16[1,16,2,1,2,4096]{5,4,2,3,0,1:T(2,128)(2,1)}), bf16[1,16,2,1,2,4096]{5,4,2,3,0,1:T(2,128)(2,1)S(1)}, u32[]{:S(2)}, u32[]{:S(2)}) async-start(bf16[1,16,2,1,2,4096]{5,4,2,3,0,1:T(2,128)(2,1)} %bitcast.52), calls=%async_computation | async-start | bytes 1048576 | tf_op jit(solution)/shard_map/all_to_all | solution.py:30
  14.2 2.5 fusion.30
  16.8 8.4 %all-to-all-done = bf16[1,16,2,1,2,4096]{5,4,2,3,0,1:T(2,128)(2,1)S(1)} async-done(((bf16[1,16,2,1,2,4096]{5,4,2,3,0,1:T(2,128)(2,1)}), bf16[1,16,2,1,2,4096]{5,4,2,3,0,1:T(2,128)(2,1)S(1)}, u32[]{:S(2)}, u32[]{:S(2)}) %all-to-all-start) | async-done | bytes 524320 | tf_op jit(solution)/shard_map/all_to_all | solution.py:30
  25.1 6.0 %all-to-all-start.2 = ((bf16[1,16,2,1,2,4096]{5,4,2,3,0,1:T(2,128)(2,1)}), bf16[1,16,2,1,2,4096]{5,4,2,3,0,1:T(2,128)(2,1)S(1)}, u32[]{:S(2)}, u32[]{:S(2)}) async-start(bf16[1,16,2,1,2,4096]{5,4,2,3,0,1:T(2,128)(2,1)} %bitcast.51), calls=%async_computation.2 | async-start | bytes 1048576 | tf_op jit(solution)/shard_map/all_to_all | solution.py:27
  31.2 7.0 %copy.38 = bf16[16,2,2,4096]{0,2,3,1:T(2,128)(2,1)} copy(bf16[16,2,2,4096]{3,2,1,0:T(2,128)(2,1)S(1)} %copy-done) | data formatting | bytes 1048576 | tf_op args[0]
  38.2 6.9 %copy.45 = bf16[16,2,2,4096]{0,2,3,1:T(2,128)(2,1)} copy(bf16[16,2,2,4096]{3,2,1,0:T(2,128)(2,1)S(1)} %copy-done.1) | data formatting | bytes 1048576 | tf_op args[1]
  45.1 35.7 %gather_fusion = bf16[4096,16,2,2]{1,3,2,0:T(2,128)(2,1)} fusion(bf16[16,2,2,4096]{0,2,3,1:T(2,128)(2,1)} %copy.38, s32[4096]{0:T(1024)S(1)} %fusion.28), kind=kCustom, calls=%fused_computation.clone | custom fusion | bytes 1064960 | tf_op jit(solution)/shard_map/jit(_take)/gather | solution.py:51
  80.8 8.3 %copy.39 = bf16[4096,16,2,2]{0,1,3,2:T(8,128)(2,1)S(1)} copy(bf16[4096,16,2,2]{1,3,2,0:T(2,128)(2,1)} %gather_fusion) | data formatting | bytes 1048576 | tf_op jit(solution)/shard_map/jit(_take)/gather | solution.py:51
  89.1 35.8 %gather_fusion.1 = bf16[4096,16,2,2]{1,3,2,0:T(2,128)(2,1)} fusion(bf16[16,2,2,4096]{0,2,3,1:T(2,128)(2,1)} %copy.45, s32[4096]{0:T(1024)S(1)} %fusion.28), kind=kCustom, calls=%fused_computation.1.clone | custom fusion | bytes 1064960 | tf_op jit(solution)/shard_map/jit(_take)/gather | solution.py:52
  124.9 9.4 %copy.46 = bf16[4096,16,2,2]{0,1,3,2:T(8,128)(2,1)} copy(bf16[4096,16,2,2]{1,3,2,0:T(2,128)(2,1)} %gather_fusion.1) | data formatting | bytes 1048576 | tf_op jit(solution)/shard_map/jit(_take)/gather | solution.py:52
  134.3 2.1 select_bitcast_fusion.1
  137.7 4.0 %all-to-all-start.1 = ((bf16[1,16,2,1,2,4096]{5,4,1,3,0,2:T(2,128)(2,1)}), bf16[1,16,2,1,2,4096]{5,4,1,3,0,2:T(2,128)(2,1)S(1)}, u32[]{:S(2)}, u32[]{:S(2)}) async-start(bf16[1,16,2,1,2,4096]{5,4,1,3,0,2:T(2,128)(2,1)} %copy.41), calls=%async_computation.1 | async-start | bytes 1048576 | tf_op jit(solution)/shard_map/all_to_all | solution.py:36
  141.7 2.2 fusion.31
  145.1 3.3 %all-to-all-done.1 = bf16[1,16,2,1,2,4096]{5,4,1,3,0,2:T(2,128)(2,1)S(1)} async-done(((bf16[1,16,2,1,2,4096]{5,4,1,3,0,2:T(2,128)(2,1)}), bf16[1,16,2,1,2,4096]{5,4,1,3,0,2:T(2,128)(2,1)S(1)}, u32[]{:S(2)}, u32[]{:S(2)}) %all-to-all-start.1) | async-done | bytes 524320 | tf_op jit(solution)/shard_map/all_to_all | solution.py:36
  148.5 5.9 %all-to-all-start.3 = ((bf16[1,16,2,1,2,4096]{5,4,1,3,0,2:T(2,128)(2,1)}), bf16[1,16,2,1,2,4096]{5,4,1,3,0,2:T(2,128)(2,1)}, u32[]{:S(2)}, u32[]{:S(2)}) async-start(bf16[1,16,2,1,2,4096]{5,4,1,3,0,2:T(2,128)(2,1)} %copy.48), calls=%async_computation.3 | async-start | bytes 1048576 | tf_op jit(solution)/shard_map/all_to_all | solution.py:35
  155.9 1.9 copy.43
  157.9 2.1 reshape.145
  160.4 3.0 %reshape.147 = bf16[1,16,2,1,2,64,64]{6,5,4,1,2,3,0:T(8,128)(2,1)} reshape(bf16[1,16,2,1,2,4096]{5,4,1,3,0,2:T(2,128)(2,1)} %all-to-all-done.3) | data formatting | bytes 1048576 | tf_op jit(solution)/shard_map/reshape | solution.py:40
  163.5 2.3 copy.49
  165.8 2.1 reshape.148
  167.9 4.3 %fusion.6 = bf16[16,2,1,4096]{3,0,2,1:T(8,128)(2,1)} fusion(f32[4096]{0:T(1024)S(1)} %mul.138, pred[16,2]{0,1:T(4,128)(4,1)S(1)} %compare_and_fusion.1, bf16[16,2,2,4096]{3,0,2,1:T(8,128)(2,1)S(1)} %reshape.148, bf16[16,2,2,4096]{3,0,2,1:T(8,128)(2,1)S(1)} %reshape.145, bf16[16,2,2,4096]{3,0,2,1:T(8,128)(2,1)} %get-tuple-element.13, ...), kind=kLoop, calls=%fused_computation.26 | loop fusion | flops 4587520 | bytes 3424288 | tf_op jit(solution)/shard_map/convert_element_type | solution.py:77
  172.2 2.1 fusion.11
  181.4 97.3 %all-reduce.3.cloned.1.call-done = f32[16,32768]{1,0:T(8,128)} async-done(((f32[16,32768]{1,0:T(8,128)}), f32[16,32768]{1,0:T(8,128)}) %all-reduce.3.cloned.1.call-update) | async-done | bytes 2097168
  278.7 2.3 fusion.27
  (51 shorter events, 14.1 us)
Async XLA Ops:
  6.5 24.6 %copy-start = (bf16[16,2,2,4096]{3,2,1,0:T(2,128)(2,1)S(1)}, bf16[16,2,2,4096]{3,2,1,0:T(2,128)(2,1)}, u32[]{:S(2)}) copy-start(bf16[16,2,2,4096]{3,2,1,0:T(2,128)(2,1)} %param.7) | copy-start | bytes 1572868
  6.5 18.6 %all-to-all-start = ((bf16[1,16,2,1,2,4096]{5,4,2,3,0,1:T(2,128)(2,1)}), bf16[1,16,2,1,2,4096]{5,4,2,3,0,1:T(2,128)(2,1)S(1)}, u32[]{:S(2)}, u32[]{:S(2)}) async-start(bf16[1,16,2,1,2,4096]{5,4,2,3,0,1:T(2,128)(2,1)} %bitcast.52), calls=%async_computation | async-start | bytes 1048576 | tf_op jit(solution)/shard_map/all_to_all | solution.py:30
  12.7 25.5 %copy-start.1 = (bf16[16,2,2,4096]{3,2,1,0:T(2,128)(2,1)S(1)}, bf16[16,2,2,4096]{3,2,1,0:T(2,128)(2,1)}, u32[]{:S(2)}) copy-start(bf16[16,2,2,4096]{3,2,1,0:T(2,128)(2,1)} %param.8) | copy-start | bytes 1572868
  25.1 112.6 %all-to-all-start.2 = ((bf16[1,16,2,1,2,4096]{5,4,2,3,0,1:T(2,128)(2,1)}), bf16[1,16,2,1,2,4096]{5,4,2,3,0,1:T(2,128)(2,1)S(1)}, u32[]{:S(2)}, u32[]{:S(2)}) async-start(bf16[1,16,2,1,2,4096]{5,4,2,3,0,1:T(2,128)(2,1)} %bitcast.51), calls=%async_computation.2 | async-start | bytes 1048576 | tf_op jit(solution)/shard_map/all_to_all | solution.py:27
  134.3 20.1 %copy-start.6 = (f32[64,64]{1,0:T(8,128)S(1)}, f32[64,64]{1,0:T(8,128)}, u32[]{:S(2)}) copy-start(f32[64,64]{1,0:T(8,128)} %param.9) | copy-start | bytes 49156
  134.3 20.2 %copy-start.7 = (s32[16]{0:T(128)S(1)}, s32[16]{0:T(128)}, u32[]{:S(2)}) copy-start(s32[16]{0:T(128)} %param.11) | copy-start | bytes 196
  137.7 10.8 %all-to-all-start.1 = ((bf16[1,16,2,1,2,4096]{5,4,1,3,0,2:T(2,128)(2,1)}), bf16[1,16,2,1,2,4096]{5,4,1,3,0,2:T(2,128)(2,1)S(1)}, u32[]{:S(2)}, u32[]{:S(2)}) async-start(bf16[1,16,2,1,2,4096]{5,4,1,3,0,2:T(2,128)(2,1)} %copy.41), calls=%async_computation.1 | async-start | bytes 1048576 | tf_op jit(solution)/shard_map/all_to_all | solution.py:36
  148.5 12.0 %all-to-all-start.3 = ((bf16[1,16,2,1,2,4096]{5,4,1,3,0,2:T(2,128)(2,1)}), bf16[1,16,2,1,2,4096]{5,4,1,3,0,2:T(2,128)(2,1)}, u32[]{:S(2)}, u32[]{:S(2)}) async-start(bf16[1,16,2,1,2,4096]{5,4,1,3,0,2:T(2,128)(2,1)} %copy.48), calls=%async_computation.3 | async-start | bytes 1048576 | tf_op jit(solution)/shard_map/all_to_all | solution.py:35
  154.4 124.3 %all-reduce.3.cloned.1.call-start = ((), (), s32[]{:S(2)}) async-start(), calls=%async_computation.4 | async-start | bytes 4194304
  167.8 4.3 %copy-start.2 = (bf16[16,2,2,4096]{3,0,2,1:T(8,128)(2,1)S(1)}, bf16[16,2,2,4096]{3,0,2,1:T(8,128)(2,1)}, u32[]{:S(2)}) copy-start(bf16[16,2,2,4096]{3,0,2,1:T(8,128)(2,1)} %get-tuple-element.12) | copy-start | bytes 1572868
  167.9 4.3 %copy-start.3 = (bf16[16,2,2,4096]{3,0,2,1:T(8,128)(2,1)S(1)}, bf16[16,2,2,4096]{3,0,2,1:T(8,128)(2,1)}, u32[]{:S(2)}) copy-start(bf16[16,2,2,4096]{3,0,2,1:T(8,128)(2,1)} %get-tuple-element.13) | copy-start | bytes 1572868
  167.9 4.3 %copy-start.4 = (bf16[16,2,1,4096]{3,2,1,0:T(2,128)(2,1)S(1)}, bf16[16,2,1,4096]{3,2,1,0:T(2,128)(2,1)}, u32[]{:S(2)}) copy-start(bf16[16,2,1,4096]{3,2,1,0:T(2,128)(2,1)} %get-tuple-element.8) | copy-start | bytes 786436
  167.9 4.3 %copy-start.5 = (bf16[16,2,1,4096]{3,2,1,0:T(2,128)(2,1)S(1)}, bf16[16,2,1,4096]{3,2,1,0:T(2,128)(2,1)}, u32[]{:S(2)}) copy-start(bf16[16,2,1,4096]{3,2,1,0:T(2,128)(2,1)} %get-tuple-element.9) | copy-start | bytes 786436
  178.7 2.0 copy-start.8
Sparse Core Ops, SparseCore 0:
  180.9 97.7 all-reduce.2
where the time goes:
time: 293 us; the launch traced here: 289 us
  local copies, waits for them, and re-layouts  130 us (44%)
  waiting for transfers between devices  110 us (38%)
  starting transfers between devices  22.1 us (8%)
  between operations  13.6 us (5%)
  other arithmetic  12.5 us (4%)
    unnamed x2, waiting for transfers between devices  97.3 us
    gather x2, local copies, waits for them, and re-layouts, per_device(): perm_lesser = jnp.take(g_lesser, permuted, axis=3)  45.2 us
    gather x2, local copies, waits for them, and re-layouts, per_device(): perm_greater = jnp.take(g_greater, permuted, axis=3)  44 us
    unnamed x21, local copies, waits for them, and re-layouts  14.6 us
    all_to_all x1, waiting for transfers between devices, per_device(): lax.all_to_all(g_lesser.reshape(layout_shape), 'col', split_axis=1, conca...  8.35 us
    all_to_all x1, starting transfers between devices, per_device(): lax.all_to_all(g_lesser.reshape(layout_shape), 'col', split_axis=1, conca...  6.15 us
    all_to_all x1, starting transfers between devices, per_device(): lax.all_to_all(g_greater.reshape(layout_shape), 'col', split_axis=1, conc...  6.02 us
    all_to_all x1, starting transfers between devices, per_device(): lax.all_to_all(half_greater, 'row', split_axis=2, concat_axis=2, tiled=True)  5.94 us
  transfers between devices with their start and end apart: 5, of which 4 were waited for; matrix products, arithmetic and copies ran while one was open for 42% of the time, Pallas kernels for 0%

commit v1 on v0

v1 whole, which is shorter than its diff:
```python
import functools
import math

import jax
import jax.numpy as jnp
from jax import lax
from jax.experimental import pallas as pl
from jax.experimental.pallas import tpu as pltpu
from jax.sharding import PartitionSpec as P

TW = 4
MESH = pl.DeviceIdType.MESH


def kernel(
    rows,
    cols,
    scaling,
    memory_ref,
    greater_ref,
    lesser_ref,
    swap_ref,
    swap_t_ref,
    weight_ref,
    out_ref,
    direct_greater,
    direct_lesser,
    mirror_greater,
    mirror_lesser,
    slab,
    total,
    direct_send,
    direct_recv,
    mirror_send,
    mirror_recv,
    slab_send,
    slab_recv,
    own_sem,
):
    row = lax.axis_index("row")
    col = lax.axis_index("col")
    orbits = greater_ref.shape[2]
    groups = cols // TW
    group = col // TW
    place = col % TW
    sources = (greater_ref, lesser_ref)
    directs = (direct_greater, direct_lesser)
    mirrors = (mirror_greater, mirror_lesser)

    barrier = pltpu.get_barrier_semaphore()

    def greet_col(step, carry):
        pl.semaphore_signal(
            barrier, inc=1, device_id=(row, lax.rem(col + step, cols)), device_id_type=MESH
        )
        return carry

    def greet_row(step, carry):
        pl.semaphore_signal(
            barrier, inc=1, device_id=(lax.rem(row + step, rows), col), device_id_type=MESH
        )
        return carry

    lax.fori_loop(1, cols, greet_col, 0)
    lax.fori_loop(1, rows, greet_row, 0)

    def own_copies():
        copies = []
        for f in range(2):
            copies.append(
                pltpu.make_async_copy(sources[f].at[col], directs[f].at[col], own_sem.at[f])
            )
            copies.append(
                pltpu.make_async_copy(
                    sources[f].at[:, row], mirrors[f].at[row], own_sem.at[2 + f]
                )
            )
        return copies

    for copy in own_copies():
        copy.start()
    pl.semaphore_wait(barrier, cols - 1 + rows - 1)

    def mirror_copy(f, other, holder):
        return pltpu.make_async_remote_copy(
            src_ref=sources[f].at[:, other],
            dst_ref=mirrors[f].at[holder],
            send_sem=mirror_send.at[f, other],
            recv_sem=mirror_recv.at[f, holder],
            device_id=(other, col),
            device_id_type=MESH,
        )

    for other in range(1, rows):
        @pl.when(other > row)
        def _(other=other):
            for f in (1, 0):
                mirror_copy(f, other, row).start()

    def direct_copy(f, target, holder):
        return pltpu.make_async_remote_copy(
            src_ref=sources[f].at[target],
            dst_ref=directs[f].at[holder],
            send_sem=direct_send.at[f, target],
            recv_sem=direct_recv.at[f, holder],
            device_id=(row, target),
            device_id_type=MESH,
        )

    def send_direct(step, carry):
        target = lax.rem(col + step, cols)
        for f in range(2):
            direct_copy(f, target, col).start()
        return carry

    lax.fori_loop(1, cols, send_direct, 0)

    def slab_copy(kind, w, k, target):
        return pltpu.make_async_remote_copy(
            src_ref=slab.at[w, k],
            dst_ref=slab.at[w, k],
            send_sem=slab_send.at[kind, k],
            recv_sem=slab_recv.at[w, k],
            device_id=(row, target),
            device_id_type=MESH,
        )

    base = group * TW
    near = base + place + 1 - 2 * lax.rem(place, 2)
    across_place = lax.rem(place + 2, TW)
    across = base + across_place
    corner_place = across_place + 1 - 2 * lax.rem(across_place, 2)
    near_place = place + 1 - 2 * lax.rem(place, 2)
    following = lax.rem(col + TW, cols)

    for copy in own_copies():
        copy.wait()

    for k in range(rows):
        @pl.when(k <= row)
        def _(k=k):
            @pl.when(k < row)
            def _():
                for f in range(2):
                    mirror_copy(f, row, k).wait_recv()

            @pl.when(group == 0)
            def _():
                copy = pltpu.make_async_copy(
                    mirror_lesser.at[k], slab.at[place, k], own_sem.at[4]
                )
                copy.start()
                copy.wait()

            @pl.when(group > 0)
            def _():
                slab_copy(0, place, k, following).wait_recv()

            @pl.when(group < groups - 1)
            def _():
                slab_copy(0, place, k, following).start()

            slab_copy(1, place, k, across).start()
            slab_copy(2, place, k, near).start()

    for k in range(rows):
        @pl.when(k <= row)
        def _(k=k):
            slab_copy(1, across_place, k, across).wait_recv()
            slab_copy(3, across_place, k, near).start()

    def wait_direct(step, carry):
        holder = lax.rem(col + step, cols)
        for f in range(2):
            direct_copy(f, holder, holder).wait_recv()
        return carry

    lax.fori_loop(1, cols, wait_direct, 0)

    for k in range(rows):
        @pl.when(k <= row)
        def _(k=k):
            slab_copy(2, near_place, k, near).wait_recv()
            slab_copy(3, corner_place, k, near).wait_recv()

    total[...] = jnp.zeros_like(total)
    swap = swap_ref[...]
    swap_t = swap_t_ref[...]
    weight = weight_ref[...]
    moment = row * cols + col
    earliest = memory_ref[col]
    lane = lax.broadcasted_iota(jnp.int32, (orbits, 2 * orbits), 1)
    half = (lane >= orbits).astype(jnp.int32)
    wide = 2 * orbits

    def energy(direct, mirrored):
        tile = direct.reshape(wide, wide)
        turned = jnp.concatenate(
            [
                jnp.concatenate([tile[:orbits, :orbits], tile[orbits:, :orbits]], axis=1),
                jnp.concatenate([tile[:orbits, orbits:], tile[orbits:, orbits:]], axis=1),
            ],
            axis=0,
        )
        swapped = jnp.dot(swap, turned, preferred_element_type=jnp.float32).astype(jnp.bfloat16)
        swapped = jnp.dot(swapped, swap_t, preferred_element_type=jnp.float32)
        back = mirrored.reshape(wide, wide).astype(jnp.float32).T
        turned = turned.astype(jnp.float32)
        ar, ai = turned[:orbits], turned[orbits:]
        br, bi = swapped[:orbits], swapped[orbits:]
        mr, mi = back[:orbits], back[orbits:]
        fr = ar * br - ai * bi
        fi = ar * bi + ai * br
        return (weight * (fr * mr - fi * mi), weight * (fr * mi + fi * mr))

    for k in range(rows):
        @pl.when(k <= row)
        def _(k=k):
            def one_pair(pair, carry):
                at = pl.ds(2 * pair, 2)
                up = energy(direct_greater[at, k], mirror_lesser[k, at])
                down = energy(direct_lesser[at, k], mirror_greater[k, at])
                second = k * cols + 2 * pair + half
                live = (second >= earliest) & (second <= moment)
                retarded = jnp.concatenate(
                    [
                        jnp.where(live, up[0] - down[0], 0.0),
                        jnp.where(live, up[1] - down[1], 0.0),
                    ],
                    axis=0,
                ).astype(jnp.bfloat16)
                for w in range(TW):
                    total[w] += jnp.dot(
                        retarded,
                        slab[w, k, at].reshape(wide, wide),
                        preferred_element_type=jnp.float32,
                    )
                return carry

            lax.fori_loop(0, cols // 2, one_pair, 0)

    for w in range(TW):
        whole = total[w]
        out_ref[w, 0] = (
            (whole[:orbits, :orbits] - whole[orbits:, orbits:]) * scaling
        ).astype(jnp.bfloat16)
        out_ref[w, 1] = (
            (whole[:orbits, orbits:] + whole[orbits:, :orbits]) * scaling
        ).astype(jnp.bfloat16)

    def drain_direct(step, carry):
        target = lax.rem(col + step, cols)
        for f in range(2):
            direct_copy(f, target, col).wait_send()
        return carry

    lax.fori_loop(1, cols, drain_direct, 0)
    for k in range(rows):
        @pl.when(k <= row)
        def _(k=k):
            @pl.when(group < groups - 1)
            def _():
                slab_copy(0, place, k, following).wait_send()

            slab_copy(1, place, k, across).wait_send()
            slab_copy(2, place, k, near).wait_send()
            slab_copy(3, across_place, k, near).wait_send()

    for other in range(1, rows):
        @pl.when(other > row)
        def _(other=other):
            for f in range(2):
                mirror_copy(f, other, row).wait_send()


def matrices(tiles, orbits):
    first, second, components, _ = tiles.shape
    return (
        tiles.reshape(first, second, components, orbits, orbits)
        .transpose(0, 1, 3, 2, 4)
        .reshape(first, second, orbits, components * orbits)
    )


def per_device(g_greater, g_lesser, coupling, partner, memory_start):
    tile_rows, tile_cols, components, pair_count = g_greater.shape
    rows = lax.axis_size("row")
    cols = lax.axis_size("col")
    orbits = coupling.shape[0]
    wide = 2 * orbits
    scaling = 1.0 / (4.0 * math.sqrt(orbits * tile_rows * rows))
    ids = jnp.arange(wide, dtype=jnp.int32)
    both = jnp.concatenate([partner, partner + orbits])
    swap = (both[:, None] == ids[None, :]).astype(jnp.bfloat16)
    swap_t = (ids[:, None] == both[None, :]).astype(jnp.bfloat16)
    weight = jnp.concatenate([coupling, coupling], axis=1)
    tile = (orbits, wide)
    vmem = pl.BlockSpec(memory_space=pltpu.VMEM)
    out = pl.pallas_call(
        functools.partial(kernel, rows, cols, scaling),
        out_shape=jax.ShapeDtypeStruct((TW, 2, orbits, orbits), jnp.bfloat16),
        in_specs=[
            pl.BlockSpec(memory_space=pltpu.SMEM),
            pl.BlockSpec(memory_space=pl.ANY),
            pl.BlockSpec(memory_space=pl.ANY),
            vmem,
            vmem,
            vmem,
        ],
        out_specs=vmem,
        scratch_shapes=[
            pltpu.VMEM((cols, rows) + tile, jnp.bfloat16),
            pltpu.VMEM((cols, rows) + tile, jnp.bfloat16),
            pltpu.VMEM((rows, cols) + tile, jnp.bfloat16),
            pltpu.VMEM((rows, cols) + tile, jnp.bfloat16),
            pltpu.VMEM((TW, rows, cols) + tile, jnp.bfloat16),
            pltpu.VMEM((TW, wide, wide), jnp.float32),
            pltpu.SemaphoreType.DMA((2, cols)),
            pltpu.SemaphoreType.DMA((2, cols)),
            pltpu.SemaphoreType.DMA((2, rows)),
            pltpu.SemaphoreType.DMA((2, rows)),
            pltpu.SemaphoreType.DMA((4, rows)),
            pltpu.SemaphoreType.DMA((TW, rows)),
            pltpu.SemaphoreType.DMA((5,)),
        ],
        compiler_params=pltpu.CompilerParams(
            collective_id=0, has_side_effects=True, vmem_limit_bytes=48 * 1024 * 1024
        ),
    )(
        memory_start,
        matrices(g_greater, orbits),
        matrices(g_lesser, orbits),
        swap,
        swap_t,
        weight,
    )
    return out.reshape(1, TW, 2, pair_count)


def solution(mesh):
    return jax.shard_map(
        per_device,
        mesh=mesh,
        in_specs=(P("row", "col", None, None), P("row", "col", None, None), P(), P(), P("row")),
        out_specs=P(("row", "col"), None, None, None),
        check_vma=False,
    )
```

time: 293 us -> 73.3 us (0.25)
  the two profiles are of different devices: /device:TPU:30 before, /device:TPU:29 now
where the time goes in v1:
time: 73.3 us; the launch traced here: 73 us
  Pallas kernels  63.9 us (87%)
  local copies, waits for them, and re-layouts  8.82 us (12%)
    pallas_call x1, Pallas kernels, per_device(): pl.pallas_call(functools.partial(kernel, rows, cols, scaling), out_shape=...  63.9 us
    reshape x4, local copies, waits for them, and re-layouts, matrices(): tiles.reshape(first, second, components, orbits, orbits)  5.11 us
    unnamed x8, local copies, waits for them, and re-layouts  1.96 us

profile of v1, /device:TPU:29, one launch (start us, length us, event | category | flops | bytes accessed | tf_op | source)
XLA Modules:
  0.0 73.0 jit_solution(3742145976775975550)
XLA Ops:
  0.0 2.3 %reshape.17 = bf16[16,2,2,64,64]{4,3,2,1,0:T(8,128)(2,1)S(1)} reshape(bf16[16,2,2,4096]{3,2,1,0:T(2,128)(2,1)} %param.5) | data formatting | bytes 1048576 | tf_op jit(solution)/shard_map/reshape | solution.py:279
  2.3 1.1 %copy.11 = bf16[16,2,2,64,64]{4,2,3,1,0:T(2,128)(2,1)S(1)} copy(bf16[16,2,2,64,64]{4,3,2,1,0:T(8,128)(2,1)S(1)} %reshape.17) | data formatting | bytes 1048576 | tf_op jit(solution)/shard_map/reshape | solution.py:279
  3.4 0.0 copy-start.1
  3.4 0.5 reshape.18.greater_ref
  3.9 0.5 copy-done.1
  4.4 0.7 reshape.19
  5.1 1.1 %copy.10 = bf16[16,2,2,64,64]{4,2,3,1,0:T(2,128)(2,1)S(1)} copy(bf16[16,2,2,64,64]{4,3,2,1,0:T(8,128)(2,1)S(1)} %reshape.19) | data formatting | bytes 1048576 | tf_op jit(solution)/shard_map/reshape | solution.py:279
  6.2 0.0 copy-start.3
  6.2 0.5 reshape.20.lesser_ref
  6.7 0.2 copy-done.3
  6.8 0.1 pad_add_fusion
  6.9 0.0 copy-start.2
  6.9 0.1 fusion.1
  7.0 0.7 copy-done.2
  7.7 0.0 copy-start
  7.7 0.1 pad_maximum_fusion.weight_ref
  7.8 0.6 copy-done
  8.3 63.9 %shard_map.55 = bf16[4,2,64,64]{3,2,1,0:T(8,128)(2,1)S(1)} custom-call(s32[16]{0:T(128)S(1)} %copy-done, bf16[16,2,64,128]{3,2,1,0:T(8,128)(2,1)S(1)} %reshape.18.greater_ref, bf16[16,2,64,128]{3,2,1,0:T(8,128)(2,1)S(1)} %reshape.20.lesser_ref, bf16[128,128]{1,0:T(8,128)(2,1)S(1)} %get-tuple-element.6.swap_ref, ...), custom_call_target="tpu_custom_call" | custom-call | tf_op jit(solution)/shard_map/pallas_call | solution.py:299
  72.2 0.8 %reshape.21 = bf16[1,4,2,4096]{3,2,1,0:T(2,128)(2,1)} reshape(bf16[4,2,64,64]{3,2,1,0:T(8,128)(2,1)S(1)} %shard_map.55) | data formatting | bytes 131072 | tf_op jit(solution)/shard_map/reshape | solution.py:337
  (1 shorter events, 0.0 us)
Async XLA Ops:
  3.4 1.0 %copy-start.1 = (bf16[16,2,2,4096]{3,2,1,0:T(2,128)(2,1)S(1)}, bf16[16,2,2,4096]{3,2,1,0:T(2,128)(2,1)}, u32[]{:S(2)}) copy-start(bf16[16,2,2,4096]{3,2,1,0:T(2,128)(2,1)} %param.6) | copy-start | bytes 1572868
  6.2 0.7 copy-start.3
  6.9 0.8 %copy-start.2 = (f32[64,64]{1,0:T(8,128)S(1)}, f32[64,64]{1,0:T(8,128)}, u32[]{:S(2)}) copy-start(f32[64,64]{1,0:T(8,128)} %param.7) | copy-start | bytes 49156
  7.7 0.7 copy-start

commit v2 on v1

v2 whole, which is shorter than its diff:
```python
import functools
import math

import jax
import jax.numpy as jnp
from jax import lax
from jax.experimental import pallas as pl
from jax.experimental.pallas import tpu as pltpu
from jax.sharding import PartitionSpec as P

TW = 4
CHUNKS = 4
MESH = pl.DeviceIdType.MESH


def kernel(
    rows,
    cols,
    scaling,
    memory_ref,
    greater_ref,
    lesser_ref,
    partner_ref,
    coupling_ref,
    out_ref,
    direct_greater,
    direct_lesser,
    mirror_greater,
    mirror_lesser,
    slab,
    transit,
    kept,
    total,
    direct_send,
    direct_recv,
    mirror_send,
    mirror_recv,
    slab_send,
    slab_recv,
    transit_send,
    transit_recv,
    own_sem,
):
    row = lax.axis_index("row")
    col = lax.axis_index("col")
    orbits = greater_ref.shape[2]
    wide = 2 * orbits
    groups = cols // TW
    group = col // TW
    place = lax.rem(col, TW)
    base = group * TW
    chunk = cols // CHUNKS
    sources = (greater_ref, lesser_ref)
    directs = (direct_greater, direct_lesser)
    mirrors = (mirror_greater, mirror_lesser)

    barrier = pltpu.get_barrier_semaphore()

    def greet_col(step, carry):
        pl.semaphore_signal(
            barrier, inc=1, device_id=(row, lax.rem(col + step, cols)), device_id_type=MESH
        )
        return carry

    def greet_row(step, carry):
        pl.semaphore_signal(
            barrier, inc=1, device_id=(lax.rem(row + step, rows), col), device_id_type=MESH
        )
        return carry

    lax.fori_loop(1, cols, greet_col, 0)
    lax.fori_loop(1, rows, greet_row, 0)

    def own_copies():
        copies = []
        for f in range(2):
            copies.append(
                pltpu.make_async_copy(sources[f].at[col], directs[f].at[col], own_sem.at[f])
            )
            copies.append(
                pltpu.make_async_copy(
                    sources[f].at[:, row], mirrors[f].at[row], own_sem.at[2 + f]
                )
            )
        return copies

    def own_slab():
        return pltpu.make_async_copy(
            lesser_ref.at[:, row], slab.at[place, row], own_sem.at[4]
        )

    for copy in own_copies():
        copy.start()

    def own_transit(other):
        return pltpu.make_async_copy(
            lesser_ref.at[:, other], transit.at[other], own_sem.at[4 + other]
        )

    @pl.when(group == 0)
    def _():
        own_slab().start()
        for other in range(1, rows):
            @pl.when(other > row)
            def _(other=other):
                own_transit(other).start()

    partners = partner_ref[...]
    partners = jnp.concatenate([partners, partners + orbits], axis=1)
    places = lax.broadcasted_iota(jnp.int32, (wide, wide), 0)
    swap_wide = jnp.where(places == partners, 1.0, 0.0)
    swap_t = swap_wide.astype(jnp.bfloat16)
    swap = swap_wide.T.astype(jnp.bfloat16)
    weight = jnp.concatenate([coupling_ref[...], coupling_ref[...]], axis=1)
    total[...] = jnp.zeros_like(total)

    pl.semaphore_wait(barrier, cols - 1 + rows - 1)

    def mirror_copy(f, other, holder):
        return pltpu.make_async_remote_copy(
            src_ref=sources[f].at[:, other],
            dst_ref=mirrors[f].at[holder],
            send_sem=mirror_send.at[f, other],
            recv_sem=mirror_recv.at[f, holder],
            device_id=(other, col),
            device_id_type=MESH,
        )

    for f in (1, 0):
        for other in range(1, rows):
            @pl.when(other > row)
            def _(other=other, f=f):
                mirror_copy(f, other, row).start()

    def direct_copy(f, target, holder, k):
        return pltpu.make_async_remote_copy(
            src_ref=sources[f].at[target, k],
            dst_ref=directs[f].at[holder, k],
            send_sem=direct_send.at[f, target, k],
            recv_sem=direct_recv.at[f, holder, k],
            device_id=(row, target),
            device_id_type=MESH,
        )

    def send_edge(target, act):
        @pl.when(target != col)
        def _():
            for f in range(2):
                act(direct_copy(f, target, col, row))

    def send_body(target, act):
        @pl.when(target != col)
        def _():
            for k in range(rows - 1):
                @pl.when(k < row)
                def _(k=k):
                    for f in range(2):
                        act(direct_copy(f, target, col, k))

    def start_edge(target, carry):
        send_edge(target, lambda copy: copy.start())
        return carry

    def start_body(target, carry):
        send_body(target, lambda copy: copy.start())
        return carry

    def slab_copy(kind, w, k, h, target):
        return pltpu.make_async_remote_copy(
            src_ref=slab.at[w, k, pl.ds(h * chunk, chunk)],
            dst_ref=slab.at[w, k, pl.ds(h * chunk, chunk)],
            send_sem=slab_send.at[kind, k, h],
            recv_sem=slab_recv.at[w, k, h],
            device_id=(row, target),
            device_id_type=MESH,
        )

    near_place = place + 1 - 2 * lax.rem(place, 2)
    across_place = lax.rem(place + 2, TW)
    corner_place = across_place + 1 - 2 * lax.rem(across_place, 2)
    near = base + near_place
    across = base + across_place
    following = lax.rem(col + TW, cols)

    def transit_copy(kind, other, h, to):
        piece = pl.ds(h * chunk, chunk)
        if kind == 0:
            return pltpu.make_async_remote_copy(
                src_ref=transit.at[other, piece],
                dst_ref=transit.at[other, piece],
                send_sem=transit_send.at[0, other, h],
                recv_sem=transit_recv.at[other, h],
                device_id=(row, following),
                device_id_type=MESH,
            )
        return pltpu.make_async_remote_copy(
            src_ref=transit.at[other, piece],
            dst_ref=slab.at[place, to, piece],
            send_sem=transit_send.at[1, other, h],
            recv_sem=slab_recv.at[place, to, h],
            device_id=(other, col),
            device_id_type=MESH,
        )

    def spread(k, h):
        slab_copy(1, place, k, h, across).start()
        slab_copy(2, place, k, h, near).start()

    def forward(copy):
        @pl.when(group < groups - 1)
        def _():
            copy.start()

    @pl.when(group == 0)
    def _():
        own_slab().wait()
        for h in range(CHUNKS):
            forward(slab_copy(0, place, row, h, following))
        for other in range(1, rows):
            @pl.when(other > row)
            def _(other=other):
                own_transit(other).wait()
                for h in range(CHUNKS):
                    forward(transit_copy(0, other, h, row))
                    transit_copy(1, other, h, row).start()
        for h in range(CHUNKS):
            spread(row, h)

    lax.fori_loop(col, cols, start_edge, 0)
    late = jnp.where(group == 0, 0, base + TW)
    lax.fori_loop(0, late, start_body, 0)

    @pl.when(group > 0)
    def _():
        for h in range(CHUNKS):
            slab_copy(0, place, row, h, following).wait_recv()
            forward(slab_copy(0, place, row, h, following))
            spread(row, h)
        for other in range(1, rows):
            @pl.when(other > row)
            def _(other=other):
                for h in range(CHUNKS):
                    transit_copy(0, other, h, row).wait_recv()
                    forward(transit_copy(0, other, h, row))
                    transit_copy(1, other, h, row).start()

    lax.fori_loop(late, cols, start_body, 0)

    def spread_again(k):
        for h in range(CHUNKS):
            slab_copy(1, across_place, k, h, across).wait_recv()
            slab_copy(3, across_place, k, h, near).start()

    spread_again(row)

    for copy in own_copies():
        copy.wait()

    moment = row * cols + col
    earliest = memory_ref[col]
    lane = lax.broadcasted_iota(jnp.int32, (orbits, wide), 1)
    half = (lane >= orbits).astype(jnp.int32)
    depth = lax.broadcasted_iota(jnp.int32, (wide, wide), 0)
    depth_half = (depth >= orbits).astype(jnp.int32)

    def energy(direct, mirrored, seen):
        tile = jnp.where(seen, direct.reshape(wide, wide).astype(jnp.float32), 0.0)
        turned = jnp.concatenate(
            [
                jnp.concatenate([tile[:orbits, :orbits], tile[orbits:, :orbits]], axis=1),
                jnp.concatenate([tile[:orbits, orbits:], tile[orbits:, orbits:]], axis=1),
            ],
            axis=0,
        )
        swapped = jnp.dot(
            swap, turned.astype(jnp.bfloat16), preferred_element_type=jnp.float32
        ).astype(jnp.bfloat16)
        swapped = jnp.dot(swapped, swap_t, preferred_element_type=jnp.float32)
        back = mirrored.reshape(wide, wide).astype(jnp.float32).T
        ar, ai = turned[:orbits], turned[orbits:]
        br, bi = swapped[:orbits], swapped[orbits:]
        mr, mi = back[:orbits], back[orbits:]
        fr = ar * br - ai * bi
        fi = ar * bi + ai * br
        return (weight * (fr * mr - fi * mi), weight * (fr * mi + fi * mr))

    def wait_direct(holder, k):
        @pl.when((holder != col) & ((k < row) | (holder <= col)))
        def _():
            for f in range(2):
                direct_copy(f, holder, holder, k).wait_recv()

    for j in range(rows):
        @pl.when(j <= row)
        def _(j=j):
            k = row - j
            if j > 0:
                for h in range(CHUNKS):
                    transit_copy(1, row, h, k).wait_recv()
                    spread(k, h)
                for f in range(2):
                    mirror_copy(f, row, k).wait_recv()
                spread_again(k)

            def one_pair(pair, carry):
                wait_direct(2 * pair, k)
                wait_direct(2 * pair + 1, k)
                at = pl.ds(2 * pair, 2)
                start = k * cols + 2 * pair
                seen = start + depth_half <= moment
                up = energy(direct_greater[at, k], mirror_lesser[k, at], seen)
                down = energy(direct_lesser[at, k], mirror_greater[k, at], seen)
                second = start + half
                live = (second >= earliest) & (second <= moment)
                kept[k, pair] = jnp.concatenate(
                    [
                        jnp.where(live, up[0] - down[0], 0.0),
                        jnp.where(live, up[1] - down[1], 0.0),
                    ],
                    axis=0,
                ).astype(jnp.bfloat16)
                return carry

            lax.fori_loop(0, jnp.where(k < row, cols // 2, col // 2 + 1), one_pair, 0)

    for j in range(rows):
        @pl.when(j <= row)
        def _(j=j):
            k = row - j
            for h in range(CHUNKS):
                slab_copy(2, near_place, k, h, near).wait_recv()
                slab_copy(3, corner_place, k, h, near).wait_recv()

            def one_product(pair, carry):
                at = pl.ds(2 * pair, 2)
                for w in range(TW):
                    total[w] += jnp.dot(
                        kept[k, pair],
                        slab[w, k, at].reshape(wide, wide),
                        preferred_element_type=jnp.float32,
                    )
                return carry

            lax.fori_loop(0, jnp.where(k < row, cols // 2, col // 2 + 1), one_product, 0)

    for w in range(TW):
        whole = total[w]
        out_ref[w, 0] = (
            (whole[:orbits, :orbits] - whole[orbits:, orbits:]) * scaling
        ).astype(jnp.bfloat16)
        out_ref[w, 1] = (
            (whole[:orbits, orbits:] + whole[orbits:, :orbits]) * scaling
        ).astype(jnp.bfloat16)

    def drain_edge(target, carry):
        send_edge(target, lambda copy: copy.wait_send())
        return carry

    def drain_body(target, carry):
        send_body(target, lambda copy: copy.wait_send())
        return carry

    lax.fori_loop(col, cols, drain_edge, 0)
    lax.fori_loop(0, cols, drain_body, 0)
    for h in range(CHUNKS):
        @pl.when(group < groups - 1)
        def _(h=h):
            slab_copy(0, place, row, h, following).wait_send()

    for k in range(rows):
        @pl.when(k <= row)
        def _(k=k):
            for h in range(CHUNKS):
                slab_copy(1, place, k, h, across).wait_send()
                slab_copy(2, place, k, h, near).wait_send()
                slab_copy(3, across_place, k, h, near).wait_send()

    for other in range(1, rows):
        @pl.when(other > row)
        def _(other=other):
            for h in range(CHUNKS):
                @pl.when(group < groups - 1)
                def _(h=h):
                    transit_copy(0, other, h, row).wait_send()

                transit_copy(1, other, h, row).wait_send()

    for other in range(1, rows):
        @pl.when(other > row)
        def _(other=other):
            for f in range(2):
                mirror_copy(f, other, row).wait_send()


def matrices(tiles, orbits):
    first, second, components, _ = tiles.shape
    return (
        tiles.reshape(first, second, components, orbits, orbits)
        .transpose(0, 1, 3, 2, 4)
        .reshape(first, second, orbits, components * orbits)
    )


def per_device(g_greater, g_lesser, coupling, partner, memory_start):
    tile_rows, tile_cols, components, pair_count = g_greater.shape
    rows = lax.axis_size("row")
    cols = lax.axis_size("col")
    orbits = coupling.shape[0]
    wide = 2 * orbits
    scaling = 1.0 / (4.0 * math.sqrt(orbits * tile_rows * rows))
    tile = (orbits, wide)
    vmem = pl.BlockSpec(memory_space=pltpu.VMEM)
    out = pl.pallas_call(
        functools.partial(kernel, rows, cols, scaling),
        out_shape=jax.ShapeDtypeStruct((TW, 2, orbits, orbits), jnp.bfloat16),
        in_specs=[
            pl.BlockSpec(memory_space=pltpu.SMEM),
            pl.BlockSpec(memory_space=pl.ANY),
            pl.BlockSpec(memory_space=pl.ANY),
            vmem,
            vmem,
        ],
        out_specs=vmem,
        scratch_shapes=[
            pltpu.VMEM((cols, rows) + tile, jnp.bfloat16),
            pltpu.VMEM((cols, rows) + tile, jnp.bfloat16),
            pltpu.VMEM((rows, cols) + tile, jnp.bfloat16),
            pltpu.VMEM((rows, cols) + tile, jnp.bfloat16),
            pltpu.VMEM((TW, rows, cols) + tile, jnp.bfloat16),
            pltpu.VMEM((rows, cols) + tile, jnp.bfloat16),
            pltpu.VMEM((rows, cols // 2, wide, wide), jnp.bfloat16),
            pltpu.VMEM((TW, wide, wide), jnp.float32),
            pltpu.SemaphoreType.DMA((2, cols, rows)),
            pltpu.SemaphoreType.DMA((2, cols, rows)),
            pltpu.SemaphoreType.DMA((2, rows)),
            pltpu.SemaphoreType.DMA((2, rows)),
            pltpu.SemaphoreType.DMA((4, rows, CHUNKS)),
            pltpu.SemaphoreType.DMA((TW, rows, CHUNKS)),
            pltpu.SemaphoreType.DMA((2, rows, CHUNKS)),
            pltpu.SemaphoreType.DMA((rows, CHUNKS)),
            pltpu.SemaphoreType.DMA((4 + rows,)),
        ],
        compiler_params=pltpu.CompilerParams(
            collective_id=0, has_side_effects=True, vmem_limit_bytes=48 * 1024 * 1024
        ),
    )(
        memory_start,
        matrices(g_greater, orbits),
        matrices(g_lesser, orbits),
        partner.reshape(1, orbits),
        coupling,
    )
    return out.reshape(1, TW, 2, pair_count)


def solution(mesh):
    return jax.shard_map(
        per_device,
        mesh=mesh,
        in_specs=(P("row", "col", None, None), P("row", "col", None, None), P(), P(), P("row")),
        out_specs=P(("row", "col"), None, None, None),
        check_vma=False,
    )
```

time: 73.3 us -> 59.3 us (0.81)
  the two profiles are of different devices: /device:TPU:29 before, /device:TPU:28 now
where the time goes in v2:
time: 59.3 us; the launch traced here: 59.1 us
  Pallas kernels  51.3 us (87%)
  local copies, waits for them, and re-layouts  7.67 us (13%)
    pallas_call x1, Pallas kernels, per_device(): pl.pallas_call(functools.partial(kernel, rows, cols, scaling), out_shape=...  51.3 us
    reshape x4, local copies, waits for them, and re-layouts, matrices(): tiles.reshape(first, second, components, orbits, orbits)  5.11 us

profile of v2, /device:TPU:28, one launch (start us, length us, event | category | flops | bytes accessed | tf_op | source)
XLA Modules:
  0.0 59.1 jit_solution(17041730109384762674)
XLA Ops:
  0.0 2.3 %reshape.18 = bf16[16,2,2,64,64]{4,3,2,1,0:T(8,128)(2,1)S(1)} reshape(bf16[16,2,2,4096]{3,2,1,0:T(2,128)(2,1)} %param.5) | data formatting | bytes 1048576 | tf_op jit(solution)/shard_map/reshape | solution.py:398
  2.3 1.1 %copy.11 = bf16[16,2,2,64,64]{4,2,3,1,0:T(2,128)(2,1)S(1)} copy(bf16[16,2,2,64,64]{4,3,2,1,0:T(8,128)(2,1)S(1)} %reshape.18) | data formatting | bytes 1048576 | tf_op jit(solution)/shard_map/reshape | solution.py:398
  3.4 0.0 copy-start.3
  3.4 0.5 reshape.19.greater_ref
  3.9 0.5 copy-done.3
  4.4 0.7 %reshape.20 = bf16[16,2,2,64,64]{4,3,2,1,0:T(8,128)(2,1)S(1)} reshape(bf16[16,2,2,4096]{3,2,1,0:T(2,128)(2,1)S(1)} %copy-done.3) | data formatting | bytes 1048576 | tf_op jit(solution)/shard_map/reshape | solution.py:398
  5.1 1.1 %copy.10 = bf16[16,2,2,64,64]{4,2,3,1,0:T(2,128)(2,1)S(1)} copy(bf16[16,2,2,64,64]{4,3,2,1,0:T(8,128)(2,1)S(1)} %reshape.20) | data formatting | bytes 1048576 | tf_op jit(solution)/shard_map/reshape | solution.py:398
  6.2 0.0 copy-start
  6.2 0.0 copy-start.1
  6.2 0.0 copy-start.2
  6.2 0.5 reshape.21.lesser_ref
  6.7 0.2 copy-done
  7.0 0.0 copy-done.1
  7.0 0.0 copy-done.2
  7.0 51.3 %shard_map.55 = bf16[4,2,64,64]{3,2,1,0:T(8,128)(2,1)S(1)} custom-call(s32[16]{0:T(128)S(1)} %copy-done.1, bf16[16,2,64,128]{3,2,1,0:T(8,128)(2,1)S(1)} %reshape.19.greater_ref, bf16[16,2,64,128]{3,2,1,0:T(8,128)(2,1)S(1)} %reshape.21.lesser_ref, s32[1,64]{1,0:T(1,128)S(1)} %bitcast.9, f32[64,64]{1,0:T(8,128)S(1)} %copy-done), custom_call_target="tpu_custom_call" | custom-call | tf_op jit(solution)/shard_map/pallas_call | solution.py:413
  58.3 0.8 %reshape.23 = bf16[1,4,2,4096]{3,2,1,0:T(2,128)(2,1)} reshape(bf16[4,2,64,64]{3,2,1,0:T(8,128)(2,1)S(1)} %shard_map.55) | data formatting | bytes 131072 | tf_op jit(solution)/shard_map/reshape | solution.py:453
Async XLA Ops:
  3.4 1.0 %copy-start.3 = (bf16[16,2,2,4096]{3,2,1,0:T(2,128)(2,1)S(1)}, bf16[16,2,2,4096]{3,2,1,0:T(2,128)(2,1)}, u32[]{:S(2)}) copy-start(bf16[16,2,2,4096]{3,2,1,0:T(2,128)(2,1)} %param.6) | copy-start | bytes 1572868
  6.2 0.8 %copy-start = (f32[64,64]{1,0:T(8,128)S(1)}, f32[64,64]{1,0:T(8,128)}, u32[]{:S(2)}) copy-start(f32[64,64]{1,0:T(8,128)} %coupling_ref.1) | copy-start | bytes 49156
  6.2 0.8 %copy-start.1 = (s32[16]{0:T(128)S(1)}, s32[16]{0:T(128)}, u32[]{:S(2)}) copy-start(s32[16]{0:T(128)} %memory_ref.1) | copy-start | bytes 196
  6.2 0.7 %copy-start.2 = (s32[64]{0:T(128)S(1)}, s32[64]{0:T(128)}, u32[]{:S(2)}) copy-start(s32[64]{0:T(128)} %param.8) | copy-start | bytes 772

commit v3 on v2

--- a/solution.py
+++ b/solution.py
@@ -9,7 +9,7 @@
 from jax.sharding import PartitionSpec as P
 
 TW = 4
-CHUNKS = 4
+CHUNKS = 8
 MESH = pl.DeviceIdType.MESH
 
 
@@ -203,8 +203,8 @@
         )
 
     def spread(k, h):
+        slab_copy(2, place, k, h, near).start()
         slab_copy(1, place, k, h, across).start()
-        slab_copy(2, place, k, h, near).start()
 
     def forward(copy):
         @pl.when(group < groups - 1)
@@ -251,7 +251,9 @@
             slab_copy(1, across_place, k, h, across).wait_recv()
             slab_copy(3, across_place, k, h, near).start()
 
-    spread_again(row)
+    @pl.when(row < rows - 1)
+    def _():
+        spread_again(row)
 
     for copy in own_copies():
         copy.wait()
@@ -322,6 +324,10 @@
                 return carry
 
             lax.fori_loop(0, jnp.where(k < row, cols // 2, col // 2 + 1), one_pair, 0)
+            if j == 0:
+                @pl.when(row == rows - 1)
+                def _():
+                    spread_again(row)
 
     for j in range(rows):
         @pl.when(j <= row)

time: 59.3 us -> 54.4 us (0.917)
  the two profiles are of different devices: /device:TPU:28 before, /device:TPU:30 now
where the time goes in v3:
time: 54.4 us; the launch traced here: 54.1 us
  Pallas kernels  46.4 us (85%)
  local copies, waits for them, and re-layouts  7.67 us (14%)
    pallas_call x1, Pallas kernels, per_device(): pl.pallas_call(functools.partial(kernel, rows, cols, scaling), out_shape=...  46.4 us
    reshape x4, local copies, waits for them, and re-layouts, matrices(): tiles.reshape(first, second, components, orbits, orbits)  5.11 us

profile of v3, /device:TPU:30, one launch (start us, length us, event | category | flops | bytes accessed | tf_op | source)
XLA Modules:
  0.0 54.1 jit_solution(15522150944148860799)
XLA Ops:
  0.0 2.3 %reshape.18 = bf16[16,2,2,64,64]{4,3,2,1,0:T(8,128)(2,1)S(1)} reshape(bf16[16,2,2,4096]{3,2,1,0:T(2,128)(2,1)} %param.5) | data formatting | bytes 1048576 | tf_op jit(solution)/shard_map/reshape | solution.py:404
  2.3 1.1 %copy.11 = bf16[16,2,2,64,64]{4,2,3,1,0:T(2,128)(2,1)S(1)} copy(bf16[16,2,2,64,64]{4,3,2,1,0:T(8,128)(2,1)S(1)} %reshape.18) | data formatting | bytes 1048576 | tf_op jit(solution)/shard_map/reshape | solution.py:404
  3.4 0.0 copy-start.3
  3.4 0.5 reshape.19.greater_ref
  3.9 0.5 %copy-done.3 = bf16[16,2,2,4096]{3,2,1,0:T(2,128)(2,1)S(1)} copy-done((bf16[16,2,2,4096]{3,2,1,0:T(2,128)(2,1)S(1)}, bf16[16,2,2,4096]{3,2,1,0:T(2,128)(2,1)}, u32[]{:S(2)}) %copy-start.3) | copy-done | bytes 524312
  4.4 0.7 %reshape.20 = bf16[16,2,2,64,64]{4,3,2,1,0:T(8,128)(2,1)S(1)} reshape(bf16[16,2,2,4096]{3,2,1,0:T(2,128)(2,1)S(1)} %copy-done.3) | data formatting | bytes 1048576 | tf_op jit(solution)/shard_map/reshape | solution.py:404
  5.1 1.1 %copy.10 = bf16[16,2,2,64,64]{4,2,3,1,0:T(2,128)(2,1)S(1)} copy(bf16[16,2,2,64,64]{4,3,2,1,0:T(8,128)(2,1)S(1)} %reshape.20) | data formatting | bytes 1048576 | tf_op jit(solution)/shard_map/reshape | solution.py:404
  6.2 0.0 copy-start
  6.2 0.0 copy-start.1
  6.2 0.0 copy-start.2
  6.2 0.5 reshape.21.lesser_ref
  6.7 0.2 copy-done
  7.0 0.0 copy-done.1
  7.0 0.0 copy-done.2
  7.0 46.4 %shard_map.55 = bf16[4,2,64,64]{3,2,1,0:T(8,128)(2,1)S(1)} custom-call(s32[16]{0:T(128)S(1)} %copy-done.1, bf16[16,2,64,128]{3,2,1,0:T(8,128)(2,1)S(1)} %reshape.19.greater_ref, bf16[16,2,64,128]{3,2,1,0:T(8,128)(2,1)S(1)} %reshape.21.lesser_ref, s32[1,64]{1,0:T(1,128)S(1)} %bitcast.9, f32[64,64]{1,0:T(8,128)S(1)} %copy-done), custom_call_target="tpu_custom_call" | custom-call | tf_op jit(solution)/shard_map/pallas_call | solution.py:419
  53.3 0.8 %reshape.23 = bf16[1,4,2,4096]{3,2,1,0:T(2,128)(2,1)} reshape(bf16[4,2,64,64]{3,2,1,0:T(8,128)(2,1)S(1)} %shard_map.55) | data formatting | bytes 131072 | tf_op jit(solution)/shard_map/reshape | solution.py:459
Async XLA Ops:
  3.4 1.0 %copy-start.3 = (bf16[16,2,2,4096]{3,2,1,0:T(2,128)(2,1)S(1)}, bf16[16,2,2,4096]{3,2,1,0:T(2,128)(2,1)}, u32[]{:S(2)}) copy-start(bf16[16,2,2,4096]{3,2,1,0:T(2,128)(2,1)} %param.6) | copy-start | bytes 1572868
  6.2 0.8 %copy-start = (f32[64,64]{1,0:T(8,128)S(1)}, f32[64,64]{1,0:T(8,128)}, u32[]{:S(2)}) copy-start(f32[64,64]{1,0:T(8,128)} %coupling_ref.1) | copy-start | bytes 49156
  6.2 0.8 %copy-start.1 = (s32[16]{0:T(128)S(1)}, s32[16]{0:T(128)}, u32[]{:S(2)}) copy-start(s32[16]{0:T(128)} %memory_ref.1) | copy-start | bytes 196
  6.2 0.7 %copy-start.2 = (s32[64]{0:T(128)S(1)}, s32[64]{0:T(128)}, u32[]{:S(2)}) copy-start(s32[64]{0:T(128)} %param.8) | copy-start | bytes 772

commit v4 on v3

--- a/solution.py
+++ b/solution.py
@@ -278,7 +278,7 @@
             swap, turned.astype(jnp.bfloat16), preferred_element_type=jnp.float32
         ).astype(jnp.bfloat16)
         swapped = jnp.dot(swapped, swap_t, preferred_element_type=jnp.float32)
-        back = mirrored.reshape(wide, wide).astype(jnp.float32).T
+        back = mirrored.reshape(wide, wide).T.astype(jnp.float32)
         ar, ai = turned[:orbits], turned[orbits:]
         br, bi = swapped[:orbits], swapped[orbits:]
         mr, mi = back[:orbits], back[orbits:]
@@ -291,6 +291,23 @@
         def _():
             for f in range(2):
                 direct_copy(f, holder, holder, k).wait_recv()
+
+    def products(k):
+        for h in range(CHUNKS):
+            slab_copy(2, near_place, k, h, near).wait_recv()
+            slab_copy(3, corner_place, k, h, near).wait_recv()
+
+        def one_product(pair, carry):
+            at = pl.ds(2 * pair, 2)
+            for w in range(TW):
+                total[w] += jnp.dot(
+                    kept[k, pair],
+                    slab[w, k, at].reshape(wide, wide),
+                    preferred_element_type=jnp.float32,
+                )
+            return carry
+
+        lax.fori_loop(0, jnp.where(k < row, cols // 2, col // 2 + 1), one_product, 0)
 
     for j in range(rows):
         @pl.when(j <= row)
@@ -303,6 +320,8 @@
                 for f in range(2):
                     mirror_copy(f, row, k).wait_recv()
                 spread_again(k)
+                if j == 1:
+                    products(row)
 
             def one_pair(pair, carry):
                 wait_direct(2 * pair, k)
@@ -330,24 +349,9 @@
                     spread_again(row)
 
     for j in range(rows):
-        @pl.when(j <= row)
+        @pl.when((j <= row) & ((j > 0) | (row == 0)))
         def _(j=j):
-            k = row - j
-            for h in range(CHUNKS):
-                slab_copy(2, near_place, k, h, near).wait_recv()
-                slab_copy(3, corner_place, k, h, near).wait_recv()
-
-            def one_product(pair, carry):
-                at = pl.ds(2 * pair, 2)
-                for w in range(TW):
-                    total[w] += jnp.dot(
-                        kept[k, pair],
-                        slab[w, k, at].reshape(wide, wide),
-                        preferred_element_type=jnp.float32,
-                    )
-                return carry
-
-            lax.fori_loop(0, jnp.where(k < row, cols // 2, col // 2 + 1), one_product, 0)
+            products(row - j)
 
     for w in range(TW):
         whole = total[w]

time: 54.4 us -> 54.4 us (level)
  no operation moved by 1% of the time
where the time goes in v4:
time: 54.4 us; the launch traced here: 54.1 us
  Pallas kernels  46.4 us (85%)
  local copies, waits for them, and re-layouts  7.67 us (14%)
    pallas_call x1, Pallas kernels, per_device(): pl.pallas_call(functools.partial(kernel, rows, cols, scaling), out_shape=...  46.4 us
    reshape x4, local copies, waits for them, and re-layouts, matrices(): tiles.reshape(first, second, components, orbits, orbits)  5.11 us

profile of v4, /device:TPU:30, one launch (start us, length us, event | category | flops | bytes accessed | tf_op | source)
XLA Modules:
  0.0 54.1 jit_solution(3164092742172932101)
XLA Ops:
  0.0 2.3 %reshape.18 = bf16[16,2,2,64,64]{4,3,2,1,0:T(8,128)(2,1)S(1)} reshape(bf16[16,2,2,4096]{3,2,1,0:T(2,128)(2,1)} %param.5) | data formatting | bytes 1048576 | tf_op jit(solution)/shard_map/reshape | solution.py:408
  2.3 1.1 %copy.11 = bf16[16,2,2,64,64]{4,2,3,1,0:T(2,128)(2,1)S(1)} copy(bf16[16,2,2,64,64]{4,3,2,1,0:T(8,128)(2,1)S(1)} %reshape.18) | data formatting | bytes 1048576 | tf_op jit(solution)/shard_map/reshape | solution.py:408
  3.4 0.0 copy-start.3
  3.4 0.5 reshape.19.greater_ref
  3.9 0.5 %copy-done.3 = bf16[16,2,2,4096]{3,2,1,0:T(2,128)(2,1)S(1)} copy-done((bf16[16,2,2,4096]{3,2,1,0:T(2,128)(2,1)S(1)}, bf16[16,2,2,4096]{3,2,1,0:T(2,128)(2,1)}, u32[]{:S(2)}) %copy-start.3) | copy-done | bytes 524312
  4.4 0.7 %reshape.20 = bf16[16,2,2,64,64]{4,3,2,1,0:T(8,128)(2,1)S(1)} reshape(bf16[16,2,2,4096]{3,2,1,0:T(2,128)(2,1)S(1)} %copy-done.3) | data formatting | bytes 1048576 | tf_op jit(solution)/shard_map/reshape | solution.py:408
  5.1 1.1 %copy.10 = bf16[16,2,2,64,64]{4,2,3,1,0:T(2,128)(2,1)S(1)} copy(bf16[16,2,2,64,64]{4,3,2,1,0:T(8,128)(2,1)S(1)} %reshape.20) | data formatting | bytes 1048576 | tf_op jit(solution)/shard_map/reshape | solution.py:408
  6.2 0.0 copy-start
  6.2 0.0 copy-start.1
  6.2 0.0 copy-start.2
  6.2 0.5 reshape.21.lesser_ref
  6.7 0.2 copy-done
  7.0 0.0 copy-done.1
  7.0 0.0 copy-done.2
  7.0 46.4 %shard_map.55 = bf16[4,2,64,64]{3,2,1,0:T(8,128)(2,1)S(1)} custom-call(s32[16]{0:T(128)S(1)} %copy-done.1, bf16[16,2,64,128]{3,2,1,0:T(8,128)(2,1)S(1)} %reshape.19.greater_ref, bf16[16,2,64,128]{3,2,1,0:T(8,128)(2,1)S(1)} %reshape.21.lesser_ref, s32[1,64]{1,0:T(1,128)S(1)} %bitcast.9, f32[64,64]{1,0:T(8,128)S(1)} %copy-done), custom_call_target="tpu_custom_call" | custom-call | tf_op jit(solution)/shard_map/pallas_call | solution.py:423
  53.3 0.8 %reshape.23 = bf16[1,4,2,4096]{3,2,1,0:T(2,128)(2,1)} reshape(bf16[4,2,64,64]{3,2,1,0:T(8,128)(2,1)S(1)} %shard_map.55) | data formatting | bytes 131072 | tf_op jit(solution)/shard_map/reshape | solution.py:463
Async XLA Ops:
  3.4 1.0 %copy-start.3 = (bf16[16,2,2,4096]{3,2,1,0:T(2,128)(2,1)S(1)}, bf16[16,2,2,4096]{3,2,1,0:T(2,128)(2,1)}, u32[]{:S(2)}) copy-start(bf16[16,2,2,4096]{3,2,1,0:T(2,128)(2,1)} %param.6) | copy-start | bytes 1572868
  6.2 0.8 %copy-start = (f32[64,64]{1,0:T(8,128)S(1)}, f32[64,64]{1,0:T(8,128)}, u32[]{:S(2)}) copy-start(f32[64,64]{1,0:T(8,128)} %coupling_ref.1) | copy-start | bytes 49156
  6.2 0.8 %copy-start.1 = (s32[16]{0:T(128)S(1)}, s32[16]{0:T(128)}, u32[]{:S(2)}) copy-start(s32[16]{0:T(128)} %memory_ref.1) | copy-start | bytes 196
  6.2 0.7 %copy-start.2 = (s32[64]{0:T(128)S(1)}, s32[64]{0:T(128)}, u32[]{:S(2)}) copy-start(s32[64]{0:T(128)} %param.8) | copy-start | bytes 772
